TPU v7x, 32 devices: a whole 2x2x4 slice. The times are simulated.
32 devices in a mesh: dp: 8 (over z, core), tensor: 4 (over y, x).
Axes of the slice: x: 2, y: 2, z: 4, core: 2. Of those that a mesh axis runs over, the one named last changes fastest.
Arguments:
- inputs: bfloat16 [49152, 512], P(('dp', 'tensor')), may hold values from -6 to 6
- w_qkv: bfloat16 [2, 3, 512, 512], P(None, None, 'dp', 'tensor'), may hold values from -0.25 to 0.25
- w_out: bfloat16 [2, 512, 512], P(None, 'tensor', 'dp'), may hold values from -0.75 to 0.75
- w_up: bfloat16 [2, 512, 2048], P(None, 'dp', 'tensor'), may hold values from -0.25 to 0.25
- w_down: bfloat16 [2, 2048, 512], P(None, 'tensor', 'dp'), may hold values from -0.125 to 0.125
- ln_gain: float32 [2, 2, 512], replicated, may hold values from 0.5 to 1.5
- ln_bias: float32 [2, 2, 512], replicated, may hold values from -3 to 3
- bias_qv: float32 [2, 2, 512], P(None, None, 'tensor'), may hold values from -3 to 3
- bias_up: float32 [2, 2048], P(None, 'tensor'), may hold values from -3 to 3
- branch_bias: float32 [2, 2, 512], replicated, may hold values from -3 to 3
- cotangent: float32 [49152, 512], P(('dp', 'tensor')), may hold values from -6 to 6
Outputs:
- outputs: bfloat16 [49152, 512], P(('dp', 'tensor'))
- input_grad: float32 [49152, 512], P(('dp', 'tensor'))
- grad_qkv: float32 [2, 3, 512, 512], P(None, None, 'dp', 'tensor')
- grad_out: float32 [2, 512, 512], P(None, 'tensor', 'dp')
- grad_up: float32 [2, 512, 2048], P(None, 'dp', 'tensor')
- grad_down: float32 [2, 2048, 512], P(None, 'tensor', 'dp')
- grad_ln_gain: float32 [2, 2, 512], replicated
- grad_ln_bias: float32 [2, 2, 512], replicated
- grad_bias_qv: float32 [2, 2, 512], P(None, None, 'tensor')
- grad_bias_up: float32 [2, 2048], P(None, 'tensor')
- grad_branch_bias: float32 [2, 2, 512], replicated
All inputs are finite; a program needn't handle non-finite values.
Results may differ from a plain program's by a relative error of at most 0.025.
Values may be sent and summed in bfloat16 or wider, within the bound.
A program may use at most 320 MiB of HBM per device.

v0:
```python
import math
import jax
import jax.numpy as jnp
from jax import lax
from jax.sharding import PartitionSpec as P

HD = 64
SPAN = 128
LEN = 2048
LAYERS = 2
highest = lax.Precision.HIGHEST
epsilon = 1e-05
masked_score = -1e30


def normalize(rows, gain, shift):
    centre = rows - jnp.mean(rows, -1, keepdims=True)
    spread = jnp.mean(centre * centre, -1, keepdims=True)
    return centre * lax.rsqrt(spread + epsilon) * gain + shift


def gelu_exact(values):
    return jax.nn.gelu(values, approximate=False)


def to_heads(rows):
    return rows.reshape(-1, LEN // SPAN, SPAN, rows.shape[1] // HD, HD)


def score_blocks(head_queries, head_keys, key_mean):
    scale = HD ** (-0.5)
    blocks = LEN // SPAN
    direct = (
        jnp.einsum(
            "gbihe,gbjhe->gbhij", head_queries, head_keys, preferred_element_type=jnp.float32
        )
        * scale
    )
    summary = jnp.einsum(
        "gbihe,gche->gbhic", head_queries.astype(jnp.float32), key_mean, precision=highest
    ) * scale + math.log(SPAN)
    inside = lax.broadcasted_iota(jnp.int32, (SPAN, SPAN), 0) >= lax.broadcasted_iota(
        jnp.int32, (SPAN, SPAN), 1
    )
    earlier = lax.broadcasted_iota(jnp.int32, (blocks, 1, 1, blocks), 0) > lax.broadcasted_iota(
        jnp.int32, (blocks, 1, 1, blocks), 3
    )
    return (jnp.where(inside, direct, masked_score), jnp.where(earlier, summary, masked_score))


def attend(query_rows, key_rows, value_rows):
    head_queries, head_keys, head_values = (
        to_heads(query_rows),
        to_heads(key_rows),
        to_heads(value_rows),
    )
    key_mean = jnp.mean(head_keys.astype(jnp.float32), 2)
    value_mean = jnp.mean(head_values.astype(jnp.float32), 2)
    direct, summary = score_blocks(head_queries, head_keys, key_mean)
    top = jnp.maximum(jnp.max(direct, -1), jnp.max(summary, -1))[..., None]
    direct_weight = jnp.exp(direct - top)
    summary_weight = jnp.exp(summary - top)
    total = jnp.sum(direct_weight, -1, keepdims=True) + jnp.sum(summary_weight, -1, keepdims=True)
    direct_prob = direct_weight / total
    summary_prob = summary_weight / total
    mixed = jnp.einsum(
        "gbhij,gbjhe->gbihe",
        direct_prob.astype(jnp.bfloat16),
        head_values,
        preferred_element_type=jnp.float32,
    )
    mixed = mixed + jnp.einsum("gbhic,gche->gbihe", summary_prob, value_mean, precision=highest)
    log_total = (top + jnp.log(total))[..., 0]
    return (mixed.reshape(query_rows.shape), log_total)


def attend_back(query_rows, key_rows, value_rows, log_total, grad_rows):
    scale = HD ** (-0.5)
    head_queries, head_keys, head_values = (
        to_heads(query_rows),
        to_heads(key_rows),
        to_heads(value_rows),
    )
    head_grads = to_heads(grad_rows)
    key_mean = jnp.mean(head_keys.astype(jnp.float32), 2)
    value_mean = jnp.mean(head_values.astype(jnp.float32), 2)
    direct, summary = score_blocks(head_queries, head_keys, key_mean)
    direct_prob = jnp.exp(direct - log_total[..., None])
    summary_prob = jnp.exp(summary - log_total[..., None])
    grad_float = head_grads.astype(jnp.float32)
    query_float = head_queries.astype(jnp.float32)
    direct_grad = jnp.einsum(
        "gbihe,gbjhe->gbhij", head_grads, head_values, preferred_element_type=jnp.float32
    )
    summary_grad = jnp.einsum("gbihe,gche->gbhic", grad_float, value_mean, precision=highest)
    centre = jnp.sum(direct_prob * direct_grad, -1, keepdims=True) + jnp.sum(
        summary_prob * summary_grad, -1, keepdims=True
    )
    direct_score = (direct_prob * (direct_grad - centre)).astype(jnp.bfloat16)
    summary_score = summary_prob * (summary_grad - centre)
    grad_query = jnp.einsum(
        "gbhij,gbjhe->gbihe", direct_score, head_keys, preferred_element_type=jnp.float32
    )
    grad_query = (
        grad_query + jnp.einsum("gbhic,gche->gbihe", summary_score, key_mean, precision=highest)
    ) * scale
    key_block = jnp.einsum("gbhic,gbihe->gche", summary_score, query_float, precision=highest) * (
        scale / SPAN
    )
    grad_key = (
        jnp.einsum(
            "gbhij,gbihe->gbjhe", direct_score, head_queries, preferred_element_type=jnp.float32
        )
        * scale
        + key_block[:, :, None]
    )
    value_block = (
        jnp.einsum("gbhic,gbihe->gche", summary_prob, grad_float, precision=highest) / SPAN
    )
    grad_value = (
        jnp.einsum(
            "gbhij,gbihe->gbjhe",
            direct_prob.astype(jnp.bfloat16),
            head_grads,
            preferred_element_type=jnp.float32,
        )
        + value_block[:, :, None]
    )
    shape = query_rows.shape
    return (grad_query.reshape(shape), grad_key.reshape(shape), grad_value.reshape(shape))


def fetch(first, second, third, fourth):
    return (
        lax.all_gather(first, "dp", axis=2, tiled=True),
        lax.all_gather(second, "dp", axis=2, tiled=True),
        lax.all_gather(third, "dp", axis=1, tiled=True),
        lax.all_gather(fourth, "dp", axis=2, tiled=True),
    )


def return_grads(first, second, third, fourth):
    return (
        lax.psum_scatter(first.astype(jnp.bfloat16), "dp", scatter_dimension=2, tiled=True).astype(
            jnp.float32
        ),
        lax.psum_scatter(second.astype(jnp.bfloat16), "dp", scatter_dimension=2, tiled=True).astype(
            jnp.float32
        ),
        lax.psum_scatter(third.astype(jnp.bfloat16), "dp", scatter_dimension=1, tiled=True).astype(
            jnp.float32
        ),
        lax.psum_scatter(fourth.astype(jnp.bfloat16), "dp", scatter_dimension=2, tiled=True).astype(
            jnp.float32
        ),
    )


def layer_weights(w_qkv, w_out, w_up, w_down, layer):
    gathered = fetch(
        w_qkv[layer : layer + 1],
        w_out[layer : layer + 1],
        w_up[layer : layer + 1],
        w_down[layer : layer + 1],
    )
    return tuple((part[0] for part in gathered))


def spread_only(rows, project):
    return project(lax.all_gather(rows, "tensor", axis=0, tiled=True))


def fold_again(rows, grads):
    return jnp.einsum(
        "td,tc->dc",
        lax.all_gather(rows, "tensor", axis=0, tiled=True),
        grads,
        preferred_element_type=jnp.float32,
    )


def spread_grads(rows, project):
    piece = lax.all_gather(rows, "tensor", axis=0, tiled=True)
    return (piece, project(piece))


def slice_term(source, weight, form):
    return jnp.einsum(form, source, weight, preferred_element_type=jnp.float32)


def rows_sum(source, weight, form):
    return lax.psum_scatter(
        slice_term(source, weight, form).astype(jnp.bfloat16),
        "tensor",
        scatter_dimension=0,
        tiled=True,
    ).astype(jnp.float32)


def grads_sum(source, weight, form):
    return lax.psum_scatter(
        slice_term(source, weight, form).astype(jnp.bfloat16),
        "tensor",
        scatter_dimension=0,
        tiled=True,
    ).astype(jnp.float32)


def group_rows(token_att, out_whole):
    groups = lax.axis_size("tensor")
    parts = token_att.reshape(token_att.shape[0], groups, -1)
    grouped = out_whole.reshape(groups, -1, out_whole.shape[1])
    partial_value = jnp.einsum("tgc,gcd->tgd", parts, grouped, preferred_element_type=jnp.float32)
    return jnp.sum(partial_value.astype(jnp.bfloat16), 1, dtype=jnp.float32)


def group_grads(token_grads, qkv_whole):
    groups = lax.axis_size("tensor")
    parts = token_grads.reshape(token_grads.shape[0], 3, groups, -1)
    grouped = qkv_whole.reshape(3, qkv_whole.shape[1], groups, -1)
    partial_value = jnp.einsum("tsgc,sdgc->tgd", parts, grouped, preferred_element_type=jnp.float32)
    return jnp.sum(partial_value.astype(jnp.bfloat16), 1, dtype=jnp.float32)


def forward_layer(residual, matrices, gains, shifts, bias_pair, bias_hidden, branch_pair):
    w_qkv, w_out, w_up, w_down = matrices
    attn_in = normalize(residual, gains[0], shifts[0]).astype(jnp.bfloat16)

    def project_qkv(piece):
        return jnp.einsum("td,sdc->tsc", piece, w_qkv, preferred_element_type=jnp.float32)

    def project_up(piece):
        return jnp.dot(piece, w_up, preferred_element_type=jnp.float32)

    mixed_qkv = spread_only(attn_in, project_qkv)
    queries = (mixed_qkv[:, 0] + bias_pair[0]).astype(jnp.bfloat16)
    keys_now = mixed_qkv[:, 1].astype(jnp.bfloat16)
    values_now = (mixed_qkv[:, 2] + bias_pair[1]).astype(jnp.bfloat16)
    mixed, log_total = attend(queries, keys_now, values_now)
    attended = mixed.astype(jnp.bfloat16)
    qkv_whole, out_whole = (
        lax.all_gather(w_qkv, "tensor", axis=2, tiled=True),
        lax.all_gather(w_out, "tensor", axis=0, tiled=True),
    )
    token_att = lax.all_to_all(attended, "tensor", split_axis=0, concat_axis=1, tiled=True)
    attn_branch = group_rows(token_att, out_whole)
    middle = residual + attn_branch + branch_pair[0]
    mlp_in = normalize(middle, gains[1], shifts[1]).astype(jnp.bfloat16)
    raised = spread_only(mlp_in, project_up)
    hidden = raised + bias_hidden
    activated = gelu_exact(hidden).astype(jnp.bfloat16)
    result = middle + rows_sum(activated, w_down, "tc,cd->td") + branch_pair[1]
    saved = (
        residual,
        middle,
        attn_in,
        mlp_in,
        None,
        None,
        queries,
        keys_now,
        values_now,
        log_total,
        attended,
        hidden,
        activated,
        qkv_whole,
    )
    return (result, saved)


def backward_layer(grad_residual, saved, matrices, gains, shifts):
    w_qkv, w_out, w_up, w_down = matrices
    (
        residual,
        middle,
        attn_in,
        mlp_in,
        attn_rows,
        mlp_rows,
        queries,
        keys_now,
        values_now,
        log_total,
        attended,
        hidden,
        activated,
        qkv_whole,
    ) = saved
    down_bias_grad = jnp.sum(grad_residual, 0)

    def back_down(piece):
        return jnp.einsum("td,fd->tf", piece, w_down, preferred_element_type=jnp.float32)

    gathered_out, grad_act = spread_grads(grad_residual.astype(jnp.bfloat16), back_down)
    down_grad = jnp.einsum("tf,td->fd", activated, gathered_out, preferred_element_type=jnp.float32)
    grad_hidden = jax.vjp(gelu_exact, hidden)[1](grad_act)[0].astype(jnp.bfloat16)
    up_bias_grad = jnp.sum(grad_hidden, 0, dtype=jnp.float32)
    up_grad = fold_again(mlp_in, grad_hidden)
    grad_mlp_in = grads_sum(grad_hidden, w_up, "tf,df->td")
    norm_back = jax.vjp(normalize, middle, gains[1], shifts[1])[1]
    grad_norm, gain_second, shift_second = norm_back(grad_mlp_in)
    grad_middle = grad_residual + grad_norm
    attn_bias_grad = jnp.sum(grad_middle, 0)

    def back_out(piece):
        return jnp.einsum("td,cd->tc", piece, w_out, preferred_element_type=jnp.float32)

    gathered_mid, grad_attended = spread_grads(grad_middle.astype(jnp.bfloat16), back_out)
    out_grad = jnp.einsum("tc,td->cd", attended, gathered_mid, preferred_element_type=jnp.float32)
    grad_query, grad_key, grad_value = attend_back(
        queries, keys_now, values_now, log_total, grad_attended.astype(jnp.bfloat16)
    )
    grad_query = grad_query.astype(jnp.bfloat16)
    grad_key = grad_key.astype(jnp.bfloat16)
    grad_value = grad_value.astype(jnp.bfloat16)
    pair_grad = jnp.stack(
        [jnp.sum(grad_query, 0, dtype=jnp.float32), jnp.sum(grad_value, 0, dtype=jnp.float32)]
    )
    stacked = jnp.stack([grad_query, grad_key, grad_value], 1)
    flat_grad = fold_again(attn_in, stacked.reshape(stacked.shape[0], -1))
    qkv_grad = jnp.transpose(flat_grad.reshape(flat_grad.shape[0], 3, -1), (1, 0, 2))
    token_grads = lax.all_to_all(stacked, "tensor", split_axis=0, concat_axis=2, tiled=True)
    grad_attn_in = group_grads(token_grads, qkv_whole)
    first_back = jax.vjp(normalize, residual, gains[0], shifts[0])[1]
    grad_first, gain_first, shift_first = first_back(grad_attn_in)
    grad_input = grad_middle + grad_first
    matrix_part = (qkv_grad[None], out_grad[None], up_grad[None], down_grad[None])
    shared_part = (
        jnp.stack([gain_first, gain_second]),
        jnp.stack([shift_first, shift_second]),
        jnp.stack([attn_bias_grad, down_bias_grad]),
    )
    head_part = (pair_grad, up_bias_grad)
    return (grad_input, matrix_part, shared_part, head_part)


def body(
    inputs, w_qkv, w_out, w_up, w_down, ln_gain, ln_bias, bias_qv, bias_up, branch_bias, cotangent
):
    residual = inputs.astype(jnp.float32)
    saved_all = []
    for layer in range(LAYERS):
        matrices = layer_weights(w_qkv, w_out, w_up, w_down, layer)
        residual, saved = forward_layer(
            residual,
            matrices,
            ln_gain[layer],
            ln_bias[layer],
            bias_qv[layer],
            bias_up[layer],
            branch_bias[layer],
        )
        saved_all.append(saved)
    outputs = residual.astype(jnp.bfloat16)
    grad_residual = cotangent
    matrix_grads = [None] * LAYERS
    shared_grads = [None] * LAYERS
    head_grads = [None] * LAYERS
    for layer in reversed(range(LAYERS)):
        matrices = layer_weights(w_qkv, w_out, w_up, w_down, layer)
        grad_residual, matrix_part, shared_part, head_part = backward_layer(
            grad_residual, saved_all[layer], matrices, ln_gain[layer], ln_bias[layer]
        )
        matrix_grads[layer] = return_grads(
            matrix_part[0], matrix_part[1], matrix_part[2], matrix_part[3]
        )
        shared_grads[layer] = shared_part
        head_grads[layer] = head_part
    joined = [jnp.concatenate([grads[index] for grads in matrix_grads], 0) for index in range(4)]
    gain_total = jnp.stack([grads[0] for grads in shared_grads])
    shift_total = jnp.stack([grads[1] for grads in shared_grads])
    branch_total = jnp.stack([grads[2] for grads in shared_grads])
    gain_sum, shift_sum, branch_sum = lax.psum(
        (gain_total, shift_total, branch_total), ("dp", "tensor")
    )
    pair_total = jnp.stack([grads[0] for grads in head_grads])
    hidden_total = jnp.stack([grads[1] for grads in head_grads])
    pair_sum, hidden_sum = lax.psum((pair_total, hidden_total), "dp")
    return (
        outputs,
        grad_residual,
        joined[0],
        joined[1],
        joined[2],
        joined[3],
        gain_sum,
        shift_sum,
        pair_sum,
        hidden_sum,
        branch_sum,
    )


def solution(mesh):
    return jax.shard_map(
        body,
        mesh=mesh,
        in_specs=(
            P(("dp", "tensor"), None),
            P(None, None, "dp", "tensor"),
            P(None, "tensor", "dp"),
            P(None, "dp", "tensor"),
            P(None, "tensor", "dp"),
            P(),
            P(),
            P(None, None, "tensor"),
            P(None, "tensor"),
            P(),
            P(("dp", "tensor"), None),
        ),
        out_specs=(
            P(("dp", "tensor"), None),
            P(("dp", "tensor"), None),
            P(None, None, "dp", "tensor"),
            P(None, "tensor", "dp"),
            P(None, "dp", "tensor"),
            P(None, "tensor", "dp"),
            P(),
            P(),
            P(None, None, "tensor"),
            P(None, "tensor"),
            P(),
        ),
        check_vma=False,
    )
```

profile of v0, /device:TPU:12, one launch (start us, length us, event | category | flops | bytes accessed | tf_op | source)
XLA Modules:
  0.0 1674.3 jit_solution(17339127591960681586)
XLA Ops:
  16.2 14.7 all_gather.71
  31.0 55.3 %all-gather.15.cloned.1.call-done = bf16[6144,512]{1,0:T(8,128)(2,1)} async-done(((bf16[1536,512]{1,0:T(8,128)(2,1)}), bf16[6144,512]{1,0:T(8,128)(2,1)}) %all-gather.15.cloned.1.call-update) | async-done | bytes 6291472 | tf_op jit(solution)/shard_map/all_gather | solution.py:170
  86.3 5.5 fusion.18
  127.3 5.7 copy.448
  132.9 6.3 reshape.482
  144.1 14.0 all_gather.72
  158.7 10.3 all-gather
  178.9 15.7 all_gather.75
  194.6 16.1 all_gather.76
  210.7 36.6 %all-gather.17.cloned.1.call-done = bf16[6144,512]{1,0:T(8,128)(2,1)} async-done(((bf16[1536,512]{1,0:T(8,128)(2,1)}), bf16[6144,512]{1,0:T(8,128)(2,1)}) %all-gather.17.cloned.1.call-update) | async-done | bytes 6291472 | tf_op jit(solution)/shard_map/all_gather | solution.py:170
  247.2 33.3 %multiply_convert_fusion.1 = (bf16[6144,512]{1,0:T(8,128)(2,1)S(1)}, f32[6144,512]{1,0:T(8,128)}, f32[6144,512]{1,0:T(8,128)}) fusion(f32[512]{0:T(512)S(1)} %bitcast.514, bf16[6144,512]{1,0:T(8,128)(2,1)} %all-gather.17.cloned.1.call-done, bf16[1,512,512]{2,1,0:T(8,128)(2,1)} %all_gather.75), kind=kOutput, calls=%fused_computation.28 | convolution fusion | flops 3428843520 | bytes 38275072 | tf_op jit(solution)/shard_map/dot_general | solution.py:233
  283.3 5.4 convolution_convert_fusion.3
  288.7 70.2 %reduce-scatter.21.cloned.1.call-done = bf16[1536,512]{1,0:T(8,128)(2,1)} async-done(((bf16[6144,512]{1,0:T(8,128)(2,1)}), bf16[1536,512]{1,0:T(8,128)(2,1)}) %reduce-scatter.21.cloned.1.call-update) | async-done | bytes 1572880 | tf_op jit(solution)/shard_map/reduce_scatter | solution.py:192
  364.4 14.9 all_gather.78
  379.3 55.4 %all-gather.19.cloned.1.call-done = bf16[6144,512]{1,0:T(8,128)(2,1)} async-done(((bf16[1536,512]{1,0:T(8,128)(2,1)}), bf16[6144,512]{1,0:T(8,128)(2,1)}) %all-gather.19.cloned.1.call-update) | async-done | bytes 6291472 | tf_op jit(solution)/shard_map/all_gather | solution.py:170
  434.7 5.5 fusion.14
  475.7 5.7 copy.449
  481.4 6.3 reshape.483
  487.7 4.9 all-to-all-start.1
  492.5 14.0 all_gather.79
  507.2 10.9 all-gather.1
  530.8 15.2 all_gather.82
  545.9 15.1 all_gather.83
  561.1 37.8 %all-gather.21.cloned.1.call-done = bf16[6144,512]{1,0:T(8,128)(2,1)} async-done(((bf16[1536,512]{1,0:T(8,128)(2,1)}), bf16[6144,512]{1,0:T(8,128)(2,1)}) %all-gather.21.cloned.1.call-update) | async-done | bytes 6291472 | tf_op jit(solution)/shard_map/all_gather | solution.py:170
  598.8 33.1 %multiply_convert_fusion = (bf16[6144,512]{1,0:T(8,128)(2,1)}, f32[6144,512]{1,0:T(8,128)}, f32[6144,512]{1,0:T(8,128)}) fusion(f32[512]{0:T(512)S(1)} %bitcast.517, bf16[6144,512]{1,0:T(8,128)(2,1)} %all-gather.21.cloned.1.call-done, bf16[1,512,512]{2,1,0:T(8,128)(2,1)S(1)} %all_gather.82), kind=kOutput, calls=%fused_computation.14 | convolution fusion | flops 3428843520 | bytes 38275072 | tf_op jit(solution)/shard_map/dot_general | solution.py:233
  631.9 38.8 %all-gather.23.cloned.1.call-done = bf16[6144,512]{1,0:T(8,128)(2,1)} async-done(((bf16[1536,512]{1,0:T(8,128)(2,1)}), bf16[6144,512]{1,0:T(8,128)(2,1)}) %all-gather.23.cloned.1.call-update) | async-done | bytes 6291472 | tf_op jit(solution)/shard_map/all_gather | solution.py:183
  670.7 14.1 convert_reduce_fusion.4
  687.5 5.4 convolution_convert_fusion.1
  693.0 8.3 convolution_convert_fusion.2
  701.7 61.4 %reduce-scatter.25.cloned.1.call-done = bf16[1536,512]{1,0:T(8,128)(2,1)} async-done(((bf16[6144,512]{1,0:T(8,128)(2,1)}), bf16[1536,512]{1,0:T(8,128)(2,1)}) %reduce-scatter.25.cloned.1.call-update) | async-done | bytes 1572880 | tf_op jit(solution)/shard_map/reduce_scatter | solution.py:201
  768.9 67.4 %reduce-scatter.23.cloned.1.call-done = bf16[1536,512]{1,0:T(8,128)(2,1)} async-done(((bf16[6144,512]{1,0:T(8,128)(2,1)}), bf16[1536,512]{1,0:T(8,128)(2,1)}) %reduce-scatter.23.cloned.1.call-update) | async-done | bytes 1572880 | tf_op jit(solution)/shard_map/reduce_scatter | solution.py:192
  836.3 5.1 fusion.269
  844.5 70.4 %all-gather.25.cloned.1.call-done = bf16[6144,512]{1,0:T(8,128)(2,1)} async-done(((bf16[1536,512]{1,0:T(8,128)(2,1)}), bf16[6144,512]{1,0:T(8,128)(2,1)}) %all-gather.25.cloned.1.call-update) | async-done | bytes 6291472 | tf_op jit(solution)/shard_map/all_gather | solution.py:183
  915.0 5.8 convolution_convert_fusion.5
  928.7 4.6 multiply_reduce_fusion.1
  945.5 6.5 multiply_convert_fusion.3
  962.9 5.2 convert_reduce_fusion.12
  976.1 10.1 copy.393
  986.2 5.8 all-to-all-start.2
  992.6 68.5 %all-gather.31.cloned.1.call-done = bf16[1,3,512,512]{3,2,1,0:T(8,128)(2,1)} async-done(((bf16[1,3,512,128]{3,2,1,0:T(8,128)(2,1)}), bf16[1,3,512,512]{3,2,1,0:T(8,128)(2,1)}) %all-gather.31.cloned.1.call-update) | async-done | bytes 1572880 | tf_op jit(solution)/shard_map/all_gather | solution.py:242
  1063.7 10.6 all-to-all-done.2
  1077.8 5.1 convert_reduce_fusion.2
  1090.3 72.9 %all-gather.27.cloned.1.call-done = bf16[6144,512]{1,0:T(8,128)(2,1)} async-done(((bf16[1536,512]{1,0:T(8,128)(2,1)}), bf16[6144,512]{1,0:T(8,128)(2,1)}) %all-gather.27.cloned.1.call-update) | async-done | bytes 6291472 | tf_op jit(solution)/shard_map/all_gather | solution.py:183
  1163.2 13.4 convert_reduce_fusion.5
  1179.3 5.3 convolution_convert_fusion
  1185.8 8.8 fusion.149
  1200.9 54.0 %reduce-scatter.27.cloned.1.call-done = bf16[1536,512]{1,0:T(8,128)(2,1)} async-done(((bf16[6144,512]{1,0:T(8,128)(2,1)}), bf16[1536,512]{1,0:T(8,128)(2,1)}) %reduce-scatter.27.cloned.1.call-update) | async-done | bytes 1572880 | tf_op jit(solution)/shard_map/reduce_scatter | solution.py:201
  1271.3 8.0 fusion.148
  1281.5 6.2 all-gather.33.cloned.1.call-done
  1293.9 8.9 fusion.147
  1302.8 14.4 reduce-scatter.43.cloned.1.call-done
  1318.3 8.9 fusion.146
  1327.2 63.8 %all-gather.29.cloned.1.call-done = bf16[6144,512]{1,0:T(8,128)(2,1)} async-done(((bf16[1536,512]{1,0:T(8,128)(2,1)}), bf16[6144,512]{1,0:T(8,128)(2,1)}) %all-gather.29.cloned.1.call-update) | async-done | bytes 6291472 | tf_op jit(solution)/shard_map/all_gather | solution.py:183
  1391.1 5.7 convolution_convert_fusion.4
  1444.5 10.2 copy.417
  1454.7 5.9 all-to-all-start.3
  1465.4 7.7 fusion.150
  1476.4 7.7 fusion.155
  1484.2 30.2 %reduce-scatter.33.cloned.1.call-done = bf16[1,64,512]{2,1,0:T(8,128)(2,1)} async-done(((bf16[1,512,512]{2,1,0:T(8,128)(2,1)}), bf16[1,64,512]{2,1,0:T(8,128)(2,1)}) %reduce-scatter.33.cloned.1.call-update) | async-done | bytes 65552 | tf_op jit(solution)/shard_map/reduce_scatter | solution.py:150
  1516.2 14.9 all-reduce.1
  1531.1 13.9 reduce-scatter.37.cloned.1.call-done
  1546.6 29.4 %reduce-scatter.31.cloned.1.call-done = bf16[1,3,64,128]{3,2,1,0:T(8,128)(2,1)} async-done(((bf16[1,3,512,128]{3,2,1,0:T(8,128)(2,1)}), bf16[1,3,64,128]{3,2,1,0:T(8,128)(2,1)}) %reduce-scatter.31.cloned.1.call-update) | async-done | bytes 49168 | tf_op jit(solution)/shard_map/reduce_scatter | solution.py:144
  1576.0 31.2 %reduce-scatter.29.cloned.1.call-done = bf16[1,3,64,128]{3,2,1,0:T(8,128)(2,1)} async-done(((bf16[1,3,512,128]{3,2,1,0:T(8,128)(2,1)}), bf16[1,3,64,128]{3,2,1,0:T(8,128)(2,1)}) %reduce-scatter.29.cloned.1.call-update) | async-done | bytes 49168 | tf_op jit(solution)/shard_map/reduce_scatter | solution.py:144
  1622.8 44.5 %all-reduce = (f32[2,2,512]{2,1,0:T(2,128)}, f32[2,2,512]{2,1,0:T(2,128)}, f32[2,2,512]{2,1,0:T(2,128)}) all-reduce(f32[2,2,512]{2,1,0:T(2,128)S(1)} %pad_maximum_fusion, f32[2,2,512]{2,1,0:T(2,128)S(1)} %pad_maximum_fusion.1, f32[2,2,512]{2,1,0:T(2,128)S(1)} %pad_maximum_fusion.2), channel_id=1, replica_groups=mesh['dp'=8,'tensor'=4] {'dp','tensor'}, use_global_device_ids=true, to_apply=%region_52.53 | all-reduce | flops 6144 | bytes 49152 | tf_op jit(solution)/shard_map/psum | solution.py:374
  (520 shorter events, 291.1 us)
Async XLA Ops:
  7.2 79.1 %all-gather.15.cloned.1.call-start = ((), (), s32[]{:S(2)}) async-start(), calls=%async_computation.16 | async-start | bytes 7864320 | tf_op jit(solution)/shard_map/all_gather | solution.py:170
  12.4 162.7 %copy-start.95 = (f32[1,1,512]{2,1,0:T(1,128)}, f32[1,1,512]{2,1,0:T(1,128)S(1)}, u32[]{:S(2)}) copy-start(f32[1,1,512]{2,1,0:T(1,128)S(1)} %get-tuple-element.137) | copy-start | bytes 6148
  15.6 92.5 %copy-start.115 = (pred[16,16]{1,0:T(8,128)(4,1)}, pred[16,16]{1,0:T(8,128)(4,1)S(1)}, u32[]{:S(2)}) copy-start(pred[16,16]{1,0:T(8,128)(4,1)S(1)} %iota_compare_fusion.1) | copy-start | bytes 772
  31.0 60.8 %copy-start.48 = (bf16[1,3,512,128]{3,2,1,0:T(8,128)(2,1)}, bf16[1,3,512,128]{3,2,1,0:T(8,128)(2,1)S(1)}, u32[]{:S(2)}) copy-start(bf16[1,3,512,128]{3,2,1,0:T(8,128)(2,1)S(1)} %all_gather.71) | copy-start | bytes 1179652
  109.0 15.5 copy-start.17
  127.2 12.0 copy-start.27
  132.9 10.5 copy-start.98
  139.2 30.0 %copy-start.112 = (f32[2,2,512]{2,1,0:T(2,128)S(1)}, f32[2,2,512]{2,1,0:T(2,128)}, u32[]{:S(2)}) copy-start(f32[2,2,512]{2,1,0:T(2,128)} %param.20) | copy-start | bytes 24580
  139.2 30.6 %all-to-all-start = ((bf16[4,1536,128]{2,1,0:T(8,128)(2,1)}), bf16[4,1536,128]{2,1,0:T(8,128)(2,1)S(1)}, u32[]{:S(2)}, u32[]{:S(2)}) async-start(bf16[4,1536,128]{2,1,0:T(8,128)(2,1)} %reshape.482), calls=%async_computation | async-start | bytes 3145728 | tf_op jit(solution)/shard_map/all_to_all | solution.py:245
  143.5 103.8 %all-gather.17.cloned.1.call-start = ((), (), s32[]{:S(2)}) async-start(), calls=%async_computation.17 | async-start | bytes 7864320 | tf_op jit(solution)/shard_map/all_gather | solution.py:170
  173.6 185.3 %copy-start = (f32[1536,512]{1,0:T(8,128)}, f32[1536,512]{1,0:T(8,128)S(1)}, u32[]{:S(2)}) copy-start(f32[1536,512]{1,0:T(8,128)S(1)} %get-tuple-element.114) | copy-start | bytes 9437188
  176.9 182.0 %reduce-scatter.21.cloned.1.call-start = ((), (), s32[]{:S(2)}) async-start(), calls=%async_computation.18 | async-start | bytes 7864320 | tf_op jit(solution)/shard_map/reduce_scatter | solution.py:192
  177.6 103.0 %copy-start.118 = (f32[1,512]{1,0:T(1,128)}, f32[1,512]{1,0:T(1,128)S(1)}, u32[]{:S(2)}) copy-start(f32[1,512]{1,0:T(1,128)S(1)} %get-tuple-element.145) | copy-start | bytes 6148
  247.2 36.1 %copy-start.58 = (bf16[1,512,512]{1,2,0:T(8,128)(2,1)S(1)}, bf16[1,512,512]{1,2,0:T(8,128)(2,1)}, u32[]{:S(2)}) copy-start(bf16[1,512,512]{1,2,0:T(8,128)(2,1)} %all_gather.76) | copy-start | bytes 1572868
  288.7 146.0 %all-gather.19.cloned.1.call-start = ((), (), s32[]{:S(2)}) async-start(), calls=%async_computation.19 | async-start | bytes 7864320 | tf_op jit(solution)/shard_map/all_gather | solution.py:170
  379.3 60.9 %copy-start.49 = (bf16[1,3,512,128]{3,2,1,0:T(8,128)(2,1)}, bf16[1,3,512,128]{3,2,1,0:T(8,128)(2,1)S(1)}, u32[]{:S(2)}) copy-start(bf16[1,3,512,128]{3,2,1,0:T(8,128)(2,1)S(1)} %all_gather.78) | copy-start | bytes 1179652
  457.3 15.6 copy-start.19
  475.7 12.0 copy-start.29
  481.4 11.1 copy-start.92
  487.7 32.7 %all-to-all-start.1 = ((bf16[4,1536,128]{2,1,0:T(8,128)(2,1)}), bf16[4,1536,128]{2,1,0:T(8,128)(2,1)}, u32[]{:S(2)}, u32[]{:S(2)}) async-start(bf16[4,1536,128]{2,1,0:T(8,128)(2,1)} %reshape.483), calls=%async_computation.2 | async-start | bytes 3145728 | tf_op jit(solution)/shard_map/all_to_all | solution.py:245
  492.5 106.3 %all-gather.21.cloned.1.call-start = ((), (), s32[]{:S(2)}) async-start(), calls=%async_computation.20 | async-start | bytes 7864320 | tf_op jit(solution)/shard_map/all_gather | solution.py:170
  527.9 18.0 %copy-start.69 = (bf16[1,512,64]{1,2,0:T(8,128)(2,1)S(1)}, bf16[1,512,64]{1,2,0:T(8,128)(2,1)}, u32[]{:S(2)}) copy-start(bf16[1,512,64]{1,2,0:T(8,128)(2,1)} %get-tuple-element.124) | copy-start | bytes 196612
  527.9 70.9 %copy-start.120 = (f32[1,512]{1,0:T(1,128)S(1)}, f32[1,512]{1,0:T(1,128)}, u32[]{:S(2)}) copy-start(f32[1,512]{1,0:T(1,128)} %get-tuple-element.144) | copy-start | bytes 6148
  527.9 142.8 %all-gather.23.cloned.1.call-start = ((), (), s32[]{:S(2)}) async-start(), calls=%async_computation.22 | async-start | bytes 7864320 | tf_op jit(solution)/shard_map/all_gather | solution.py:183
  530.7 232.4 %reduce-scatter.25.cloned.1.call-start = ((), (), s32[]{:S(2)}) async-start(), calls=%async_computation.23 | async-start | bytes 7864320 | tf_op jit(solution)/shard_map/reduce_scatter | solution.py:201
  692.9 143.4 %reduce-scatter.23.cloned.1.call-start = ((), (), s32[]{:S(2)}) async-start(), calls=%async_computation.21 | async-start | bytes 7864320 | tf_op jit(solution)/shard_map/reduce_scatter | solution.py:192
  701.2 61.9 %copy-start.6 = (f32[1536,512]{1,0:T(8,128)S(1)}, f32[1536,512]{1,0:T(8,128)}, u32[]{:S(2)}) copy-start(f32[1536,512]{1,0:T(8,128)} %copy-done.5) | copy-start | bytes 9437188
  701.3 213.7 %all-gather.25.cloned.1.call-start = ((), (), s32[]{:S(2)}) async-start(), calls=%async_computation.24 | async-start | bytes 7864320 | tf_op jit(solution)/shard_map/all_gather | solution.py:183
  766.4 69.9 %copy-start.107 = (f32[1,1,512]{2,1,0:T(1,128)S(1)}, f32[1,1,512]{2,1,0:T(1,128)}, u32[]{:S(2)}) copy-start(f32[1,1,512]{2,1,0:T(1,128)} %get-tuple-element.132) | copy-start | bytes 6148
  843.1 71.9 %copy-start.56 = (bf16[1,128,512]{1,2,0:T(8,128)(2,1)S(1)}, bf16[1,128,512]{1,2,0:T(8,128)(2,1)}, u32[]{:S(2)}) copy-start(bf16[1,128,512]{1,2,0:T(8,128)(2,1)} %copy-done.55) | copy-start | bytes 393220
  920.8 7.9 slice-start.2
  945.5 6.5 copy-start.24
  986.2 88.0 %all-to-all-start.2 = ((bf16[6144,3,128]{2,1,0:T(4,128)(2,1)}), bf16[6144,3,128]{2,1,0:T(4,128)(2,1)}, u32[]{:S(2)}, u32[]{:S(2)}) async-start(bf16[6144,3,128]{2,1,0:T(4,128)(2,1)} %copy.393), calls=%async_computation.5 | async-start | bytes 12582912 | tf_op jit(solution)/shard_map/all_to_all | solution.py:323
  992.0 69.1 %all-gather.31.cloned.1.call-start = ((), (), s32[]{:S(2)}) async-start(), calls=%async_computation.32 | async-start | bytes 1966080 | tf_op jit(solution)/shard_map/all_gather | solution.py:242
  992.6 170.6 %all-gather.27.cloned.1.call-start = ((), (), s32[]{:S(2)}) async-start(), calls=%async_computation.25 | async-start | bytes 7864320 | tf_op jit(solution)/shard_map/all_gather | solution.py:183
  1088.9 74.3 %copy-start.59 = (bf16[1,512,512]{1,2,0:T(8,128)(2,1)S(1)}, bf16[1,512,512]{1,2,0:T(8,128)(2,1)}, u32[]{:S(2)}) copy-start(bf16[1,512,512]{1,2,0:T(8,128)(2,1)} %all_gather.76) | copy-start | bytes 1572868
  1088.9 74.3 %copy-start.119 = (f32[1,512]{1,0:T(1,128)S(1)}, f32[1,512]{1,0:T(1,128)}, u32[]{:S(2)}) copy-start(f32[1,512]{1,0:T(1,128)} %copy-done.118) | copy-start | bytes 6148
  1090.2 164.6 %reduce-scatter.27.cloned.1.call-start = ((), (), s32[]{:S(2)}) async-start(), calls=%async_computation.26 | async-start | bytes 7864320 | tf_op jit(solution)/shard_map/reduce_scatter | solution.py:201
  1163.2 16.1 copy-start.57
  1184.6 103.1 %all-gather.33.cloned.1.call-start = ((), (), s32[]{:S(2)}) async-start(), calls=%async_computation.33 | async-start | bytes 1966080 | tf_op jit(solution)/shard_map/all_gather | solution.py:242
  1185.4 131.8 %reduce-scatter.43.cloned.1.call-start = ((), (), s32[]{:S(2)}) async-start(), calls=%async_computation.37 | async-start | bytes 589824
  1194.7 60.2 %copy-start.1 = (f32[1536,512]{1,0:T(8,128)S(1)}, f32[1536,512]{1,0:T(8,128)}, u32[]{:S(2)}) copy-start(f32[1536,512]{1,0:T(8,128)} %copy-done) | copy-start | bytes 9437188
  1194.7 60.2 %copy-start.67 = (f32[1536]{0:T(1024)S(1)}, f32[1536]{0:T(1024)}, u32[]{:S(2)}) copy-start(f32[1536]{0:T(1024)} %copy-done.66) | copy-start | bytes 18436
  1194.7 60.2 %copy-start.96 = (f32[1,1,512]{2,1,0:T(1,128)S(1)}, f32[1,1,512]{2,1,0:T(1,128)}, u32[]{:S(2)}) copy-start(f32[1,1,512]{2,1,0:T(1,128)} %copy-done.95) | copy-start | bytes 6148
  1198.4 59.1 %copy-start.89 = (f32[1536]{0:T(1024)S(1)}, f32[1536]{0:T(1024)}, u32[]{:S(2)}) copy-start(f32[1536]{0:T(1024)} %copy-done.88) | copy-start | bytes 18436
  1198.4 59.2 %copy-start.80 = (f32[1536]{0:T(1024)S(1)}, f32[1536]{0:T(1024)}, u32[]{:S(2)}) copy-start(f32[1536]{0:T(1024)} %copy-done.79) | copy-start | bytes 18436
  1200.8 190.2 %all-gather.29.cloned.1.call-start = ((), (), s32[]{:S(2)}) async-start(), calls=%async_computation.27 | async-start | bytes 7864320 | tf_op jit(solution)/shard_map/all_gather | solution.py:183
  1264.2 209.2 %reduce-scatter.39.cloned.1.call-start = ((), (), s32[]{:S(2)}) async-start(), calls=%async_computation.35 | async-start | bytes 147456
  1271.3 203.1 %reduce-scatter.41.cloned.1.call-start = ((), (), s32[]{:S(2)}) async-start(), calls=%async_computation.36 | async-start | bytes 589824
  1279.4 11.9 copy-start.28
  1281.3 11.0 copy-start.51
  1281.3 202.9 %reduce-scatter.35.cloned.1.call-start = ((), (), s32[]{:S(2)}) async-start(), calls=%async_computation.31 | async-start | bytes 589824 | tf_op jit(solution)/shard_map/reduce_scatter | solution.py:150
  1302.8 211.6 %reduce-scatter.33.cloned.1.call-start = ((), (), s32[]{:S(2)}) async-start(), calls=%async_computation.30 | async-start | bytes 589824 | tf_op jit(solution)/shard_map/reduce_scatter | solution.py:150
  1318.3 72.8 %copy-start.54 = (bf16[1,128,512]{1,2,0:T(8,128)(2,1)S(1)}, bf16[1,128,512]{1,2,0:T(8,128)(2,1)}, u32[]{:S(2)}) copy-start(bf16[1,128,512]{1,2,0:T(8,128)(2,1)} %copy-done.53) | copy-start | bytes 393220
  1396.8 8.1 slice-start
  1454.7 154.0 %all-to-all-start.3 = ((bf16[6144,3,128]{2,1,0:T(4,128)(2,1)}), bf16[6144,3,128]{2,1,0:T(4,128)(2,1)}, u32[]{:S(2)}, u32[]{:S(2)}) async-start(bf16[6144,3,128]{2,1,0:T(4,128)(2,1)} %copy.417), calls=%async_computation.7 | async-start | bytes 12582912 | tf_op jit(solution)/shard_map/all_to_all | solution.py:323
  1460.6 84.4 %reduce-scatter.37.cloned.1.call-start = ((), (), s32[]{:S(2)}) async-start(), calls=%async_computation.34 | async-start | bytes 147456
  1465.3 7.8 copy-start.122
  1465.3 7.9 copy-start.123
  1465.3 8.9 copy-start.117
  1465.3 110.7 %reduce-scatter.31.cloned.1.call-start = ((), (), s32[]{:S(2)}) async-start(), calls=%async_computation.29 | async-start | bytes 442368 | tf_op jit(solution)/shard_map/reduce_scatter | solution.py:144
  1473.3 133.8 %reduce-scatter.29.cloned.1.call-start = ((), (), s32[]{:S(2)}) async-start(), calls=%async_computation.28 | async-start | bytes 442368 | tf_op jit(solution)/shard_map/reduce_scatter | solution.py:144
  1476.4 39.6 %copy-start.103 = (f32[512]{0:T(512)S(1)}, f32[512]{0:T(512)}, u32[]{:S(2)}) copy-start(f32[512]{0:T(512)} %get-tuple-element.121) | copy-start | bytes 6148
  1476.4 39.6 %copy-start.104 = (f32[512]{0:T(512)S(1)}, f32[512]{0:T(512)}, u32[]{:S(2)}) copy-start(f32[512]{0:T(512)} %get-tuple-element.95) | copy-start | bytes 6148
  (95 other events, 291.1 us)
Sparse Core Ops, SparseCore 0:
  15.0 71.2 all-gather.14
  177.1 70.1 all-gather.16
  288.8 70.0 reduce-scatter.20
  364.3 70.3 all-gather.18
  528.0 70.7 all-gather.20
  600.5 70.1 all-gather.22
  693.0 70.0 reduce-scatter.24
  766.1 70.1 reduce-scatter.22
  844.6 70.3 all-gather.24
  994.3 66.7 all-gather.30
  1090.4 72.8 all-gather.26
  1184.8 70.0 reduce-scatter.26
  1256.7 30.9 all-gather.32
  1289.8 27.3 reduce-scatter.42
  1319.1 71.9 all-gather.28
  1393.8 26.6 reduce-scatter.38
  1422.6 28.9 reduce-scatter.40
  1453.8 29.1 reduce-scatter.34
  1485.3 29.0 reduce-scatter.32
  1516.5 28.3 reduce-scatter.36
  1547.2 28.7 reduce-scatter.30
  1578.4 28.7 reduce-scatter.28
where the time goes:
time: 1690 us; the launch traced here: 1670 us
  waiting for transfers between devices  890 us (53%)
  matrix products  278 us (16%)
  blocking collectives  200 us (12%)
  local copies, waits for them, and re-layouts  189 us (11%)
  other arithmetic  78.1 us (5%)
  starting transfers between devices  22.5 us (1%)
    all_gather x4, waiting for transfers between devices, spread_grads(): piece = lax.all_gather(rows, 'tensor', axis=0, tiled=True)  246 us
    all_gather x4, waiting for transfers between devices, spread_only(): return project(lax.all_gather(rows, 'tensor', axis=0, tiled=True))  185 us
    reduce_scatter x2, waiting for transfers between devices, rows_sum(): lax.psum_scatter(slice_term(source, weight, form).astype(jnp.bfloat16), '...  138 us
    reduce_scatter x2, waiting for transfers between devices, grads_sum(): lax.psum_scatter(slice_term(source, weight, form).astype(jnp.bfloat16), '...  115 us
    all_gather x2, waiting for transfers between devices, forward_layer(): lax.all_gather(w_qkv, 'tensor', axis=2, tiled=True)  74.7 us
    dot_general x2, matrix products, project_up(): return jnp.dot(piece, w_up, preferred_element_type=jnp.float32)  66.4 us
    reduce_scatter x2, waiting for transfers between devices, return_grads(): lax.psum_scatter(first.astype(jnp.bfloat16), 'dp', scatter_dimension=2, t...  60.6 us
    unnamed x296, local copies, waits for them, and re-layouts  59.3 us
  transfers between devices with their start and end apart: 26, of which 20 were waited for; matrix products, arithmetic and copies ran while one was open for 13% of the time, Pallas kernels for 0%

commit v1 on v0

--- a/solution.py
+++ b/solution.py
@@ -11,6 +11,23 @@
 highest = lax.Precision.HIGHEST
 epsilon = 1e-05
 masked_score = -1e30
+
+
+def core_scan(xx):
+    slots = lax.axis_size("tensor")
+    buffers = list(map(lambda it: (it, (it + 1) % slots), range(slots)))
+    y = map(lambda it: (it, (it - 1) % slots), range(slots))
+    xs_all = list(y)
+    view_out, u_next = ([xx], [xx])
+    for _ in range(slots // 2):
+        built = lax.ppermute(view_out[-1], axis_name="tensor", perm=buffers)
+        view_out.append(built)
+    i0 = 0
+    while i0 < (slots - 1) // 2:
+        u_next.append(lax.ppermute(u_next[-1], axis_name="tensor", perm=xs_all))
+        i0 += 1
+    state_next = jnp.concatenate([*view_out[::-1], *u_next[1:]], 0)
+    return jnp.roll(state_next, (lax.axis_index("tensor") - slots // 2) * xx.shape[0], 0)
 
 
 def normalize(rows, gain, shift):
@@ -167,7 +184,7 @@
 
 
 def spread_only(rows, project):
-    return project(lax.all_gather(rows, "tensor", axis=0, tiled=True))
+    return project(core_scan(rows))
 
 
 def fold_again(rows, grads):

time: 1690 us -> 2200 us (1.30)
  waiting for transfers between devices: 890 us -> 1310 us
  matrix products: 278 us -> 359 us
    ppermute x0 -> x12, waiting for transfers between devices: none -> 353 us  [the longest x8 300 us: core_scan(): built = lax.ppermute(view_out[-1], axis_name='tensor', perm=buffers)]
    unnamed x26, waiting for transfers between devices: 29.9 us -> 87.7 us
    dot_general x2, matrix products: 66.4 us -> 111 us  [project_up(): return jnp.dot(piece, w_up, preferred_element_type=jnp.float32)]
    all_gather x4, waiting for transfers between devices: 246 us -> 207 us  [spread_grads(): piece = lax.all_gather(rows, 'tensor', axis=0, tiled=True)]
    dot_general x2, matrix products: 11 us -> 47.7 us  [project_qkv(): jnp.einsum('td,sdc->tsc', piece, w_qkv, preferred_element_type=jnp.float32)]
    all_gather x4, waiting for transfers between devices: 185 us -> 210 us  [fold_again(): lax.all_gather(rows, 'tensor', axis=0, tiled=True)]
    reduce_scatter x2, waiting for transfers between devices: 30.2 us -> 53.4 us  [return_grads(): lax.psum_scatter(third.astype(jnp.bfloat16), 'dp', scatter_dimension=1, t...]
    unnamed x296 -> x320, local copies, waits for them, and re-layouts: 59.3 us -> 58.5 us
  transfers between devices with their start and end apart: 26 -> 38, of which waited for: 20 -> 33; matrix products, arithmetic and copies ran while one was open for 13% -> 11% of each run, Pallas kernels for 0% -> 0%
where the time goes in v1:
time: 2200 us; the launch traced here: 2190 us
  waiting for transfers between devices  1310 us (60%)
  matrix products  359 us (16%)
  local copies, waits for them, and re-layouts  198 us (9%)
  blocking collectives  198 us (9%)
  other arithmetic  75.7 us (3%)
  starting transfers between devices  34.2 us (2%)
    ppermute x8, waiting for transfers between devices, core_scan(): built = lax.ppermute(view_out[-1], axis_name='tensor', perm=buffers)  300 us
    all_gather x4, waiting for transfers between devices, fold_again(): lax.all_gather(rows, 'tensor', axis=0, tiled=True)  210 us
    all_gather x4, waiting for transfers between devices, spread_grads(): piece = lax.all_gather(rows, 'tensor', axis=0, tiled=True)  207 us
    reduce_scatter x2, waiting for transfers between devices, rows_sum(): lax.psum_scatter(slice_term(source, weight, form).astype(jnp.bfloat16), '...  138 us
    reduce_scatter x2, waiting for transfers between devices, grads_sum(): lax.psum_scatter(slice_term(source, weight, form).astype(jnp.bfloat16), '...  114 us
    dot_general x2, matrix products, project_up(): return jnp.dot(piece, w_up, preferred_element_type=jnp.float32)  111 us
    unnamed x26, waiting for transfers between devices  87.7 us
    all_gather x2, waiting for transfers between devices, forward_layer(): lax.all_gather(w_qkv, 'tensor', axis=2, tiled=True)  74.2 us
  transfers between devices with their start and end apart: 38, of which 33 were waited for; matrix products, arithmetic and copies ran while one was open for 11% of the time, Pallas kernels for 0%

profile of v1, /device:TPU:12, one launch (start us, length us, event | category | flops | bytes accessed | tf_op | source)
XLA Modules:
  0.0 2189.6 jit_solution(9094403434782645555)
XLA Ops:
  16.1 35.4 %collective-permute-done = bf16[1536,512]{1,0:T(8,128)(2,1)} collective-permute-done((bf16[1536,512]{1,0:T(8,128)(2,1)S(1)}, bf16[1536,512]{1,0:T(8,128)(2,1)}, u32[]{:S(2)}, u32[]{:S(2)}) %collective-permute-start) | collective-permute-done | bytes 1572896 | tf_op jit(solution)/shard_map/ppermute | solution.py:23
  53.5 14.8 all_gather.66
  68.2 16.0 collective-permute-done.2
  84.2 33.5 %collective-permute-done.1 = bf16[1536,512]{1,0:T(8,128)(2,1)} collective-permute-done((bf16[1536,512]{1,0:T(8,128)(2,1)}, bf16[1536,512]{1,0:T(8,128)(2,1)}, u32[]{:S(2)}, u32[]{:S(2)}) %collective-permute-start.1) | collective-permute-done | bytes 1572896 | tf_op jit(solution)/shard_map/ppermute | solution.py:23
  117.7 24.1 %fusion.48 = f32[6144,3,128]{2,0,1:T(8,128)} fusion(s32[]{:T(128)S(6)} %select_n.39, bf16[1536,512]{1,0:T(8,128)(2,1)} %collective-permute-done.1, bf16[1536,512]{1,0:T(8,128)(2,1)} %collective-permute-done, bf16[1536,512]{1,0:T(8,128)(2,1)S(1)} %fusion.75, bf16[1536,512]{1,0:T(8,128)(2,1)} %collective-permute-done.2, ...), kind=kOutput, calls=%fused_computation.112 | convolution fusion | flops 2466250752 | bytes 16121860 | tf_op jit(solution)/shard_map/td,sdc->tsc/dot_general | solution.py:247
  141.8 6.0 fusion.322
  187.8 6.3 reshape.482
  198.5 14.2 all_gather.67
  213.3 10.3 all-gather
  234.9 35.5 %collective-permute-done.3 = bf16[1536,512]{1,0:T(8,128)(2,1)S(1)} collective-permute-done((bf16[1536,512]{1,0:T(8,128)(2,1)}, bf16[1536,512]{1,0:T(8,128)(2,1)S(1)}, u32[]{:S(2)}, u32[]{:S(2)}) %collective-permute-start.3) | collective-permute-done | bytes 1572896 | tf_op jit(solution)/shard_map/ppermute | solution.py:23
  272.3 15.3 all_gather.69
  287.6 15.0 all_gather.70
  303.3 32.5 %collective-permute-done.4 = bf16[1536,512]{1,0:T(8,128)(2,1)S(1)} collective-permute-done((bf16[1536,512]{1,0:T(8,128)(2,1)S(1)}, bf16[1536,512]{1,0:T(8,128)(2,1)S(1)}, u32[]{:S(2)}, u32[]{:S(2)}) %collective-permute-start.4) | collective-permute-done | bytes 1572896 | tf_op jit(solution)/shard_map/ppermute | solution.py:23
  335.8 59.4 %multiply_convert_fusion.1 = (bf16[6144,512]{1,0:T(8,128)(2,1)S(1)}, f32[6144,512]{1,0:T(8,128)}, f32[6144,512]{1,0:T(8,128)}) fusion(f32[512]{0:T(512)S(1)} %bitcast.512, bf16[1,512,512]{2,1,0:T(8,128)(2,1)S(1)} %all_gather.69, s32[]{:T(128)S(6)} %select_n.39, bf16[1536,512]{1,0:T(8,128)(2,1)S(1)} %collective-permute-done.4, ...), kind=kOutput, calls=%fused_computation.60 | convolution fusion | flops 3479175168 | bytes 38275076 | tf_op jit(solution)/shard_map/dot_general | solution.py:250
  403.2 70.3 %reduce-scatter.21.cloned.1.call-done = bf16[1536,512]{1,0:T(8,128)(2,1)} async-done(((bf16[6144,512]{1,0:T(8,128)(2,1)}), bf16[1536,512]{1,0:T(8,128)(2,1)}) %reduce-scatter.21.cloned.1.call-update) | async-done | bytes 1572880 | tf_op jit(solution)/shard_map/reduce_scatter | solution.py:209
  480.6 35.4 %collective-permute-done.6 = bf16[1536,512]{1,0:T(8,128)(2,1)} collective-permute-done((bf16[1536,512]{1,0:T(8,128)(2,1)S(1)}, bf16[1536,512]{1,0:T(8,128)(2,1)}, u32[]{:S(2)}, u32[]{:S(2)}) %collective-permute-start.6) | collective-permute-done | bytes 1572896 | tf_op jit(solution)/shard_map/ppermute | solution.py:23
  516.2 14.5 all_gather.71
  530.7 18.3 collective-permute-done.8
  549.0 33.3 %collective-permute-done.7 = bf16[1536,512]{1,0:T(8,128)(2,1)} collective-permute-done((bf16[1536,512]{1,0:T(8,128)(2,1)}, bf16[1536,512]{1,0:T(8,128)(2,1)}, u32[]{:S(2)}, u32[]{:S(2)}) %collective-permute-start.7) | collective-permute-done | bytes 1572896 | tf_op jit(solution)/shard_map/ppermute | solution.py:23
  582.3 23.7 %fusion.27 = f32[6144,3,128]{2,0,1:T(8,128)} fusion(s32[]{:T(128)S(6)} %select_n.39, bf16[1536,512]{1,0:T(8,128)(2,1)} %collective-permute-done.7, bf16[1536,512]{1,0:T(8,128)(2,1)} %collective-permute-done.6, bf16[1536,512]{1,0:T(8,128)(2,1)S(1)} %add_convert_fusion.10, bf16[1536,512]{1,0:T(8,128)(2,1)} %collective-permute-done.8, ...), kind=kOutput, calls=%fused_computation.95 | convolution fusion | flops 2466250752 | bytes 16121860 | tf_op jit(solution)/shard_map/td,sdc->tsc/dot_general | solution.py:247
  605.9 5.9 fusion.321
  652.1 6.3 reshape.483
  663.0 14.0 all_gather.72
  677.6 10.9 all-gather.1
  701.8 35.6 %collective-permute-done.9 = bf16[1536,512]{1,0:T(8,128)(2,1)} collective-permute-done((bf16[1536,512]{1,0:T(8,128)(2,1)}, bf16[1536,512]{1,0:T(8,128)(2,1)}, u32[]{:S(2)}, u32[]{:S(2)}) %collective-permute-start.9) | collective-permute-done | bytes 1572896 | tf_op jit(solution)/shard_map/ppermute | solution.py:23
  740.1 14.9 all_gather.74
  755.0 14.9 all_gather.75
  769.9 17.9 collective-permute-done.11
  787.8 58.7 %collective-permute-done.10 = bf16[1536,512]{1,0:T(8,128)(2,1)} collective-permute-done((bf16[1536,512]{1,0:T(8,128)(2,1)}, bf16[1536,512]{1,0:T(8,128)(2,1)}, u32[]{:S(2)}, u32[]{:S(2)}) %collective-permute-start.10) | collective-permute-done | bytes 1572896 | tf_op jit(solution)/shard_map/ppermute | solution.py:23
  846.5 51.1 %multiply_convert_fusion = (bf16[6144,512]{1,0:T(8,128)(2,1)}, f32[6144,512]{1,0:T(8,128)}, f32[6144,512]{1,0:T(8,128)}) fusion(f32[512]{0:T(512)S(1)} %bitcast.515, bf16[1,512,512]{2,1,0:T(8,128)(2,1)S(1)} %all_gather.74, s32[]{:T(128)S(6)} %select_n.39, bf16[1536,512]{1,0:T(8,128)(2,1)} %collective-permute-done.10, ...), kind=kOutput, calls=%fused_computation.46 | convolution fusion | flops 3479175168 | bytes 38275076 | tf_op jit(solution)/shard_map/dot_general | solution.py:250
  897.7 14.0 convert_reduce_fusion.4
  919.7 8.6 convolution_convert_fusion.2
  928.4 61.4 %reduce-scatter.25.cloned.1.call-done = bf16[1536,512]{1,0:T(8,128)(2,1)} async-done(((bf16[6144,512]{1,0:T(8,128)(2,1)}), bf16[1536,512]{1,0:T(8,128)(2,1)}) %reduce-scatter.25.cloned.1.call-update) | async-done | bytes 1572880 | tf_op jit(solution)/shard_map/reduce_scatter | solution.py:218
  995.6 67.2 %reduce-scatter.23.cloned.1.call-done = bf16[1536,512]{1,0:T(8,128)(2,1)} async-done(((bf16[6144,512]{1,0:T(8,128)(2,1)}), bf16[1536,512]{1,0:T(8,128)(2,1)}) %reduce-scatter.23.cloned.1.call-update) | async-done | bytes 1572880 | tf_op jit(solution)/shard_map/reduce_scatter | solution.py:209
  1071.1 70.4 %all-gather.17.cloned.1.call-done = bf16[6144,512]{1,0:T(8,128)(2,1)} async-done(((bf16[1536,512]{1,0:T(8,128)(2,1)}), bf16[6144,512]{1,0:T(8,128)(2,1)}) %all-gather.17.cloned.1.call-update) | async-done | bytes 6291472 | tf_op jit(solution)/shard_map/all_gather | solution.py:200
  1172.1 6.5 multiply_convert_fusion.3
  1202.7 10.2 copy.393
  1219.3 68.5 %all-gather.31.cloned.1.call-done = bf16[1,3,512,512]{3,2,1,0:T(8,128)(2,1)} async-done(((bf16[1,3,512,128]{3,2,1,0:T(8,128)(2,1)}), bf16[1,3,512,512]{3,2,1,0:T(8,128)(2,1)}) %all-gather.31.cloned.1.call-update) | async-done | bytes 1572880 | tf_op jit(solution)/shard_map/all_gather | solution.py:259
  1290.4 10.6 all-to-all-done.2
  1317.0 72.9 %all-gather.19.cloned.1.call-done = bf16[6144,512]{1,0:T(8,128)(2,1)} async-done(((bf16[1536,512]{1,0:T(8,128)(2,1)}), bf16[6144,512]{1,0:T(8,128)(2,1)}) %all-gather.19.cloned.1.call-update) | async-done | bytes 6291472 | tf_op jit(solution)/shard_map/all_gather | solution.py:200
  1390.0 13.6 convert_reduce_fusion.5
  1413.4 8.8 fusion.187
  1428.9 52.9 %reduce-scatter.27.cloned.1.call-done = bf16[1536,512]{1,0:T(8,128)(2,1)} async-done(((bf16[6144,512]{1,0:T(8,128)(2,1)}), bf16[1536,512]{1,0:T(8,128)(2,1)}) %reduce-scatter.27.cloned.1.call-update) | async-done | bytes 1572880 | tf_op jit(solution)/shard_map/reduce_scatter | solution.py:218
  1498.3 8.0 fusion.186
  1520.9 65.7 %all-gather.29.cloned.1.call-done = bf16[6144,512]{1,0:T(8,128)(2,1)} async-done(((bf16[1536,512]{1,0:T(8,128)(2,1)}), bf16[6144,512]{1,0:T(8,128)(2,1)}) %all-gather.29.cloned.1.call-update) | async-done | bytes 6291472 | tf_op jit(solution)/shard_map/all_gather | solution.py:193
  1586.6 8.8 fusion.185
  1595.5 20.8 reduce-scatter.43.cloned.1.call-done
  1617.3 72.7 %all-gather.27.cloned.1.call-done = bf16[6144,512]{1,0:T(8,128)(2,1)} async-done(((bf16[1536,512]{1,0:T(8,128)(2,1)}), bf16[6144,512]{1,0:T(8,128)(2,1)}) %all-gather.27.cloned.1.call-update) | async-done | bytes 6291472 | tf_op jit(solution)/shard_map/all_gather | solution.py:193
  1690.0 8.8 fusion.184
  1698.9 63.3 %all-gather.21.cloned.1.call-done = bf16[6144,512]{1,0:T(8,128)(2,1)} async-done(((bf16[1536,512]{1,0:T(8,128)(2,1)}), bf16[6144,512]{1,0:T(8,128)(2,1)}) %all-gather.21.cloned.1.call-update) | async-done | bytes 6291472 | tf_op jit(solution)/shard_map/all_gather | solution.py:200
  1815.6 10.2 copy.417
  1825.8 5.9 all-to-all-start.3
  1836.5 7.7 fusion.188
  1844.5 19.3 reduce-scatter.39.cloned.1.call-done
  1864.7 30.3 %reduce-scatter.41.cloned.1.call-done = bf16[64,512]{1,0:T(8,128)(2,1)} async-done(((bf16[512,512]{1,0:T(8,128)(2,1)}), bf16[64,512]{1,0:T(8,128)(2,1)}) %reduce-scatter.41.cloned.1.call-update) | async-done | bytes 65552
  1897.0 71.8 %all-gather.23.cloned.1.call-done = bf16[6144,512]{1,0:T(8,128)(2,1)} async-done(((bf16[1536,512]{1,0:T(8,128)(2,1)}), bf16[6144,512]{1,0:T(8,128)(2,1)}) %all-gather.23.cloned.1.call-update) | async-done | bytes 6291472 | tf_op jit(solution)/shard_map/all_gather | solution.py:193
  1968.8 7.7 fusion.193
  1976.5 21.9 reduce-scatter.35.cloned.1.call-done
  1998.4 31.5 %reduce-scatter.33.cloned.1.call-done = bf16[1,64,512]{2,1,0:T(8,128)(2,1)} async-done(((bf16[1,512,512]{2,1,0:T(8,128)(2,1)}), bf16[1,64,512]{2,1,0:T(8,128)(2,1)}) %reduce-scatter.33.cloned.1.call-update) | async-done | bytes 65552 | tf_op jit(solution)/shard_map/reduce_scatter | solution.py:167
  2031.7 14.9 all-reduce.1
  2046.6 13.8 reduce-scatter.37.cloned.1.call-done
  2061.9 29.4 %reduce-scatter.31.cloned.1.call-done = bf16[1,3,64,128]{3,2,1,0:T(8,128)(2,1)} async-done(((bf16[1,3,512,128]{3,2,1,0:T(8,128)(2,1)}), bf16[1,3,64,128]{3,2,1,0:T(8,128)(2,1)}) %reduce-scatter.31.cloned.1.call-update) | async-done | bytes 49168 | tf_op jit(solution)/shard_map/reduce_scatter | solution.py:161
  2091.4 31.2 %reduce-scatter.29.cloned.1.call-done = bf16[1,3,64,128]{3,2,1,0:T(8,128)(2,1)} async-done(((bf16[1,3,512,128]{3,2,1,0:T(8,128)(2,1)}), bf16[1,3,64,128]{3,2,1,0:T(8,128)(2,1)}) %reduce-scatter.29.cloned.1.call-update) | async-done | bytes 49168 | tf_op jit(solution)/shard_map/reduce_scatter | solution.py:161
  2138.1 44.4 %all-reduce = (f32[2,2,512]{2,1,0:T(2,128)}, f32[2,2,512]{2,1,0:T(2,128)}, f32[2,2,512]{2,1,0:T(2,128)}) all-reduce(f32[2,2,512]{2,1,0:T(2,128)S(1)} %pad_maximum_fusion, f32[2,2,512]{2,1,0:T(2,128)S(1)} %pad_maximum_fusion.1, f32[2,2,512]{2,1,0:T(2,128)S(1)} %pad_maximum_fusion.2), channel_id=1, replica_groups=mesh['dp'=8,'tensor'=4] {'dp','tensor'}, use_global_device_ids=true, to_apply=%region_52.54 | all-reduce | flops 6144 | bytes 49152 | tf_op jit(solution)/shard_map/psum | solution.py:391
  (568 shorter events, 375.4 us)
Async XLA Ops:
  11.8 217.9 %copy-start.104 = (f32[1,1,512]{2,1,0:T(1,128)}, f32[1,1,512]{2,1,0:T(1,128)S(1)}, u32[]{:S(2)}) copy-start(f32[1,1,512]{2,1,0:T(1,128)S(1)} %get-tuple-element.138) | copy-start | bytes 6148
  13.1 128.7 %copy-start.35 = (bf16[1536,512]{1,0:T(8,128)(2,1)}, bf16[1536,512]{1,0:T(8,128)(2,1)S(1)}, u32[]{:S(2)}) copy-start(bf16[1536,512]{1,0:T(8,128)(2,1)S(1)} %fusion.75) | copy-start | bytes 4718596
  13.1 38.3 %collective-permute-start = (bf16[1536,512]{1,0:T(8,128)(2,1)S(1)}, bf16[1536,512]{1,0:T(8,128)(2,1)}, u32[]{:S(2)}, u32[]{:S(2)}) collective-permute-start(bf16[1536,512]{1,0:T(8,128)(2,1)S(1)} %fusion.75), channel_id=1, source_target_pairs={{0,1},{1,2},{2,3},{3,0},{4,5},{5,6},{6,7},{7,4},{8,9},{9,10},{10,1... | collective-permute-start | bytes 4718600 | tf_op jit(solution)/shard_map/ppermute | solution.py:23
  14.7 69.5 %collective-permute-start.2 = (bf16[1536,512]{1,0:T(8,128)(2,1)S(1)}, bf16[1536,512]{1,0:T(8,128)(2,1)}, u32[]{:S(2)}, u32[]{:S(2)}) collective-permute-start(bf16[1536,512]{1,0:T(8,128)(2,1)S(1)} %fusion.75), channel_id=1, source_target_pairs={{0,3},{1,0},{2,1},{3,2},{4,7},{5,4},{6,5},{7,6},{8,11},{9,8},{10,9... | collective-permute-start | bytes 4718600 | tf_op jit(solution)/shard_map/ppermute | solution.py:27
  51.5 66.3 %collective-permute-start.1 = (bf16[1536,512]{1,0:T(8,128)(2,1)}, bf16[1536,512]{1,0:T(8,128)(2,1)}, u32[]{:S(2)}, u32[]{:S(2)}) collective-permute-start(bf16[1536,512]{1,0:T(8,128)(2,1)} %collective-permute-done), channel_id=1, source_target_pairs={{0,1},{1,2},{2,3},{3,0},{4,5},{5,6},{6,7},{7,4},{8,9},{9,10},{10,1... | collective-permute-start | bytes 4718600 | tf_op jit(solution)/shard_map/ppermute | solution.py:23
  52.8 110.2 %copy-start.127 = (pred[16,16]{1,0:T(8,128)(4,1)}, pred[16,16]{1,0:T(8,128)(4,1)S(1)}, u32[]{:S(2)}) copy-start(pred[16,16]{1,0:T(8,128)(4,1)S(1)} %iota_compare_fusion.1) | copy-start | bytes 772
  52.9 108.5 %copy-start.111 = (pred[128,128]{0,1:T(8,128)(4,1)}, pred[128,128]{0,1:T(8,128)(4,1)S(1)}, u32[]{:S(2)}) copy-start(pred[128,128]{0,1:T(8,128)(4,1)S(1)} %iota_compare_fusion) | copy-start | bytes 49156
  68.2 73.6 %copy-start.51 = (bf16[1,3,512,128]{3,2,1,0:T(8,128)(2,1)}, bf16[1,3,512,128]{3,2,1,0:T(8,128)(2,1)S(1)}, u32[]{:S(2)}) copy-start(bf16[1,3,512,128]{3,2,1,0:T(8,128)(2,1)S(1)} %all_gather.66) | copy-start | bytes 1179652
  194.1 30.3 %all-to-all-start = ((bf16[4,1536,128]{2,1,0:T(8,128)(2,1)}), bf16[4,1536,128]{2,1,0:T(8,128)(2,1)S(1)}, u32[]{:S(2)}, u32[]{:S(2)}) async-start(bf16[4,1536,128]{2,1,0:T(8,128)(2,1)} %reshape.482), calls=%async_computation | async-start | bytes 3145728 | tf_op jit(solution)/shard_map/all_to_all | solution.py:262
  197.8 275.7 %reduce-scatter.21.cloned.1.call-start = ((), (), s32[]{:S(2)}) async-start(), calls=%async_computation.16 | async-start | bytes 7864320 | tf_op jit(solution)/shard_map/reduce_scatter | solution.py:209
  228.1 245.4 %copy-start = (f32[1536,512]{1,0:T(8,128)}, f32[1536,512]{1,0:T(8,128)S(1)}, u32[]{:S(2)}) copy-start(f32[1536,512]{1,0:T(8,128)S(1)} %get-tuple-element.115) | copy-start | bytes 9437188
  232.0 38.4 %collective-permute-start.3 = (bf16[1536,512]{1,0:T(8,128)(2,1)}, bf16[1536,512]{1,0:T(8,128)(2,1)S(1)}, u32[]{:S(2)}, u32[]{:S(2)}) collective-permute-start(bf16[1536,512]{1,0:T(8,128)(2,1)} %add_convert_fusion.11), channel_id=1, source_target_pairs={{0,1},{1,2},{2,3},{3,0},{4,5},{5,6},{6,7},{7,4},{8,9},{9,10},{10,1... | collective-permute-start | bytes 4718600 | tf_op jit(solution)/shard_map/ppermute | solution.py:23
  232.6 70.7 %collective-permute-start.5 = (bf16[1536,512]{1,0:T(8,128)(2,1)}, bf16[1536,512]{1,0:T(8,128)(2,1)S(1)}, u32[]{:S(2)}, u32[]{:S(2)}) collective-permute-start(bf16[1536,512]{1,0:T(8,128)(2,1)} %add_convert_fusion.11), channel_id=1, source_target_pairs={{0,3},{1,0},{2,1},{3,2},{4,7},{5,4},{6,5},{7,6},{8,11},{9,8},{10,9... | collective-permute-start | bytes 4718600 | tf_op jit(solution)/shard_map/ppermute | solution.py:27
  270.5 65.3 %collective-permute-start.4 = (bf16[1536,512]{1,0:T(8,128)(2,1)S(1)}, bf16[1536,512]{1,0:T(8,128)(2,1)S(1)}, u32[]{:S(2)}, u32[]{:S(2)}) collective-permute-start(bf16[1536,512]{1,0:T(8,128)(2,1)S(1)} %collective-permute-done.3), channel_id=1, source_target_pairs={{0,1},{1,2},{2,3},{3,0},{4,5},{5,6},{6,7},{7,4},{8,9},{9,10},{10,1... | collective-permute-start | bytes 4718600 | tf_op jit(solution)/shard_map/ppermute | solution.py:23
  271.1 124.1 %copy-start.130 = (f32[1,512]{1,0:T(1,128)}, f32[1,512]{1,0:T(1,128)S(1)}, u32[]{:S(2)}) copy-start(f32[1,512]{1,0:T(1,128)S(1)} %get-tuple-element.146) | copy-start | bytes 6148
  287.6 107.5 %copy-start.59 = (bf16[1,512,512]{2,1,0:T(8,128)(2,1)}, bf16[1,512,512]{2,1,0:T(8,128)(2,1)S(1)}, u32[]{:S(2)}) copy-start(bf16[1,512,512]{2,1,0:T(8,128)(2,1)S(1)} %all_gather.69) | copy-start | bytes 1572868
  302.6 92.5 %copy-start.61 = (bf16[1,512,512]{1,2,0:T(8,128)(2,1)}, bf16[1,512,512]{1,2,0:T(8,128)(2,1)S(1)}, u32[]{:S(2)}) copy-start(bf16[1,512,512]{1,2,0:T(8,128)(2,1)S(1)} %all_gather.70) | copy-start | bytes 1572868
  477.7 128.3 %copy-start.44 = (bf16[1536,512]{1,0:T(8,128)(2,1)}, bf16[1536,512]{1,0:T(8,128)(2,1)S(1)}, u32[]{:S(2)}) copy-start(bf16[1536,512]{1,0:T(8,128)(2,1)S(1)} %add_convert_fusion.10) | copy-start | bytes 4718596
  477.7 38.3 %collective-permute-start.6 = (bf16[1536,512]{1,0:T(8,128)(2,1)S(1)}, bf16[1536,512]{1,0:T(8,128)(2,1)}, u32[]{:S(2)}, u32[]{:S(2)}) collective-permute-start(bf16[1536,512]{1,0:T(8,128)(2,1)S(1)} %add_convert_fusion.10), channel_id=1, source_target_pairs={{0,1},{1,2},{2,3},{3,0},{4,5},{5,6},{6,7},{7,4},{8,9},{9,10},{10,1... | collective-permute-start | bytes 4718600 | tf_op jit(solution)/shard_map/ppermute | solution.py:23
  478.4 70.5 %collective-permute-start.8 = (bf16[1536,512]{1,0:T(8,128)(2,1)S(1)}, bf16[1536,512]{1,0:T(8,128)(2,1)}, u32[]{:S(2)}, u32[]{:S(2)}) collective-permute-start(bf16[1536,512]{1,0:T(8,128)(2,1)S(1)} %add_convert_fusion.10), channel_id=1, source_target_pairs={{0,3},{1,0},{2,1},{3,2},{4,7},{5,4},{6,5},{7,6},{8,11},{9,8},{10,9... | collective-permute-start | bytes 4718600 | tf_op jit(solution)/shard_map/ppermute | solution.py:27
  516.0 66.3 %collective-permute-start.7 = (bf16[1536,512]{1,0:T(8,128)(2,1)}, bf16[1536,512]{1,0:T(8,128)(2,1)}, u32[]{:S(2)}, u32[]{:S(2)}) collective-permute-start(bf16[1536,512]{1,0:T(8,128)(2,1)} %collective-permute-done.6), channel_id=1, source_target_pairs={{0,1},{1,2},{2,3},{3,0},{4,5},{5,6},{6,7},{7,4},{8,9},{9,10},{10,1... | collective-permute-start | bytes 4718600 | tf_op jit(solution)/shard_map/ppermute | solution.py:23
  530.7 75.3 %copy-start.52 = (bf16[1,3,512,128]{3,2,1,0:T(8,128)(2,1)}, bf16[1,3,512,128]{3,2,1,0:T(8,128)(2,1)S(1)}, u32[]{:S(2)}) copy-start(bf16[1,3,512,128]{3,2,1,0:T(8,128)(2,1)S(1)} %all_gather.71) | copy-start | bytes 1179652
  658.4 32.4 %all-to-all-start.1 = ((bf16[4,1536,128]{2,1,0:T(8,128)(2,1)}), bf16[4,1536,128]{2,1,0:T(8,128)(2,1)}, u32[]{:S(2)}, u32[]{:S(2)}) async-start(bf16[4,1536,128]{2,1,0:T(8,128)(2,1)} %reshape.483), calls=%async_computation.2 | async-start | bytes 3145728 | tf_op jit(solution)/shard_map/all_to_all | solution.py:262
  663.0 234.7 %all-gather.15.cloned.1.call-start = ((), (), s32[]{:S(2)}) async-start(), calls=%async_computation.18 | async-start | bytes 7864320 | tf_op jit(solution)/shard_map/all_gather | solution.py:200
  698.9 147.6 %copy-start.132 = (f32[1,512]{1,0:T(1,128)S(1)}, f32[1,512]{1,0:T(1,128)}, u32[]{:S(2)}) copy-start(f32[1,512]{1,0:T(1,128)} %get-tuple-element.145) | copy-start | bytes 6148
  698.9 38.5 %collective-permute-start.9 = (bf16[1536,512]{1,0:T(8,128)(2,1)}, bf16[1536,512]{1,0:T(8,128)(2,1)}, u32[]{:S(2)}, u32[]{:S(2)}) collective-permute-start(bf16[1536,512]{1,0:T(8,128)(2,1)} %add_convert_fusion.7), channel_id=1, source_target_pairs={{0,1},{1,2},{2,3},{3,0},{4,5},{5,6},{6,7},{7,4},{8,9},{9,10},{10,1... | collective-permute-start | bytes 4718600 | tf_op jit(solution)/shard_map/ppermute | solution.py:23
  700.1 87.6 %collective-permute-start.11 = (bf16[1536,512]{1,0:T(8,128)(2,1)}, bf16[1536,512]{1,0:T(8,128)(2,1)}, u32[]{:S(2)}, u32[]{:S(2)}) collective-permute-start(bf16[1536,512]{1,0:T(8,128)(2,1)} %add_convert_fusion.7), channel_id=1, source_target_pairs={{0,3},{1,0},{2,1},{3,2},{4,7},{5,4},{6,5},{7,6},{8,11},{9,8},{10,9... | collective-permute-start | bytes 4718600 | tf_op jit(solution)/shard_map/ppermute | solution.py:27
  737.4 109.0 %collective-permute-start.10 = (bf16[1536,512]{1,0:T(8,128)(2,1)}, bf16[1536,512]{1,0:T(8,128)(2,1)}, u32[]{:S(2)}, u32[]{:S(2)}) collective-permute-start(bf16[1536,512]{1,0:T(8,128)(2,1)} %collective-permute-done.9), channel_id=1, source_target_pairs={{0,1},{1,2},{2,3},{3,0},{4,5},{5,6},{6,7},{7,4},{8,9},{9,10},{10,1... | collective-permute-start | bytes 4718600 | tf_op jit(solution)/shard_map/ppermute | solution.py:23
  740.1 249.7 %reduce-scatter.25.cloned.1.call-start = ((), (), s32[]{:S(2)}) async-start(), calls=%async_computation.19 | async-start | bytes 7864320 | tf_op jit(solution)/shard_map/reduce_scatter | solution.py:218
  919.7 143.2 %reduce-scatter.23.cloned.1.call-start = ((), (), s32[]{:S(2)}) async-start(), calls=%async_computation.17 | async-start | bytes 7864320 | tf_op jit(solution)/shard_map/reduce_scatter | solution.py:209
  928.3 61.5 %copy-start.6 = (f32[1536,512]{1,0:T(8,128)S(1)}, f32[1536,512]{1,0:T(8,128)}, u32[]{:S(2)}) copy-start(f32[1536,512]{1,0:T(8,128)} %copy-done.5) | copy-start | bytes 9437188
  928.3 61.5 %copy-start.72 = (f32[1536]{0:T(1024)S(1)}, f32[1536]{0:T(1024)}, u32[]{:S(2)}) copy-start(f32[1536]{0:T(1024)} %copy-done.71) | copy-start | bytes 18436
  928.3 61.5 %copy-start.107 = (f32[1,1,512]{2,1,0:T(1,128)S(1)}, f32[1,1,512]{2,1,0:T(1,128)}, u32[]{:S(2)}) copy-start(f32[1,1,512]{2,1,0:T(1,128)} %get-tuple-element.137) | copy-start | bytes 6148
  928.3 64.8 %copy-start.100 = (f32[1536]{0:T(1024)S(1)}, f32[1536]{0:T(1024)}, u32[]{:S(2)}) copy-start(f32[1536]{0:T(1024)} %copy-done.99) | copy-start | bytes 18436
  928.3 64.8 %copy-start.87 = (f32[1536]{0:T(1024)S(1)}, f32[1536]{0:T(1024)}, u32[]{:S(2)}) copy-start(f32[1536]{0:T(1024)} %copy-done.86) | copy-start | bytes 18436
  928.3 213.2 %all-gather.17.cloned.1.call-start = ((), (), s32[]{:S(2)}) async-start(), calls=%async_computation.20 | async-start | bytes 7864320 | tf_op jit(solution)/shard_map/all_gather | solution.py:200
  993.1 69.8 %copy-start.119 = (f32[1,1,512]{2,1,0:T(1,128)S(1)}, f32[1,1,512]{2,1,0:T(1,128)}, u32[]{:S(2)}) copy-start(f32[1,1,512]{2,1,0:T(1,128)} %get-tuple-element.133) | copy-start | bytes 6148
  1069.7 71.9 %copy-start.58 = (bf16[1,128,512]{1,2,0:T(8,128)(2,1)S(1)}, bf16[1,128,512]{1,2,0:T(8,128)(2,1)}, u32[]{:S(2)}) copy-start(bf16[1,128,512]{1,2,0:T(8,128)(2,1)} %copy-done.57) | copy-start | bytes 393220
  1212.9 88.0 %all-to-all-start.2 = ((bf16[6144,3,128]{2,1,0:T(4,128)(2,1)}), bf16[6144,3,128]{2,1,0:T(4,128)(2,1)}, u32[]{:S(2)}, u32[]{:S(2)}) async-start(bf16[6144,3,128]{2,1,0:T(4,128)(2,1)} %copy.393), calls=%async_computation.5 | async-start | bytes 12582912 | tf_op jit(solution)/shard_map/all_to_all | solution.py:340
  1218.7 69.1 %all-gather.31.cloned.1.call-start = ((), (), s32[]{:S(2)}) async-start(), calls=%async_computation.32 | async-start | bytes 1966080 | tf_op jit(solution)/shard_map/all_gather | solution.py:259
  1219.2 170.7 %all-gather.19.cloned.1.call-start = ((), (), s32[]{:S(2)}) async-start(), calls=%async_computation.21 | async-start | bytes 7864320 | tf_op jit(solution)/shard_map/all_gather | solution.py:200
  1315.6 74.4 %copy-start.62 = (bf16[1,512,512]{1,2,0:T(8,128)(2,1)S(1)}, bf16[1,512,512]{1,2,0:T(8,128)(2,1)}, u32[]{:S(2)}) copy-start(bf16[1,512,512]{1,2,0:T(8,128)(2,1)} %copy-done.61) | copy-start | bytes 1572868
  1315.6 74.4 %copy-start.131 = (f32[1,512]{1,0:T(1,128)S(1)}, f32[1,512]{1,0:T(1,128)}, u32[]{:S(2)}) copy-start(f32[1,512]{1,0:T(1,128)} %copy-done.130) | copy-start | bytes 6148
  1317.0 164.9 %reduce-scatter.27.cloned.1.call-start = ((), (), s32[]{:S(2)}) async-start(), calls=%async_computation.22 | async-start | bytes 7864320 | tf_op jit(solution)/shard_map/reduce_scatter | solution.py:218
  1411.6 103.1 %all-gather.33.cloned.1.call-start = ((), (), s32[]{:S(2)}) async-start(), calls=%async_computation.33 | async-start | bytes 1966080 | tf_op jit(solution)/shard_map/all_gather | solution.py:259
  1412.4 174.2 %all-gather.29.cloned.1.call-start = ((), (), s32[]{:S(2)}) async-start(), calls=%async_computation.30 | async-start | bytes 7864320 | tf_op jit(solution)/shard_map/all_gather | solution.py:193
  1413.0 203.3 %reduce-scatter.43.cloned.1.call-start = ((), (), s32[]{:S(2)}) async-start(), calls=%async_computation.37 | async-start | bytes 589824
  1422.3 59.6 %copy-start.70 = (f32[1536]{0:T(1024)S(1)}, f32[1536]{0:T(1024)}, u32[]{:S(2)}) copy-start(f32[1536]{0:T(1024)} %copy-done.69) | copy-start | bytes 18436
  1422.3 59.6 %copy-start.105 = (f32[1,1,512]{2,1,0:T(1,128)S(1)}, f32[1,1,512]{2,1,0:T(1,128)}, u32[]{:S(2)}) copy-start(f32[1,1,512]{2,1,0:T(1,128)} %copy-done.104) | copy-start | bytes 6148
  1428.3 261.7 %all-gather.27.cloned.1.call-start = ((), (), s32[]{:S(2)}) async-start(), calls=%async_computation.28 | async-start | bytes 7864320 | tf_op jit(solution)/shard_map/all_gather | solution.py:193
  1428.9 333.4 %all-gather.21.cloned.1.call-start = ((), (), s32[]{:S(2)}) async-start(), calls=%async_computation.23 | async-start | bytes 7864320 | tf_op jit(solution)/shard_map/all_gather | solution.py:200
  1491.2 345.3 %all-gather.25.cloned.1.call-start = ((), (), s32[]{:S(2)}) async-start(), calls=%async_computation.26 | async-start | bytes 7864320 | tf_op jit(solution)/shard_map/all_gather | solution.py:193
  1491.8 372.0 %reduce-scatter.39.cloned.1.call-start = ((), (), s32[]{:S(2)}) async-start(), calls=%async_computation.35 | async-start | bytes 147456
  1498.3 396.7 %reduce-scatter.41.cloned.1.call-start = ((), (), s32[]{:S(2)}) async-start(), calls=%async_computation.36 | async-start | bytes 589824
  1508.2 460.6 %all-gather.23.cloned.1.call-start = ((), (), s32[]{:S(2)}) async-start(), calls=%async_computation.24 | async-start | bytes 7864320 | tf_op jit(solution)/shard_map/all_gather | solution.py:193
  1508.8 489.6 %reduce-scatter.35.cloned.1.call-start = ((), (), s32[]{:S(2)}) async-start(), calls=%async_computation.31 | async-start | bytes 589824 | tf_op jit(solution)/shard_map/reduce_scatter | solution.py:167
  1595.4 434.4 %reduce-scatter.33.cloned.1.call-start = ((), (), s32[]{:S(2)}) async-start(), calls=%async_computation.29 | async-start | bytes 589824 | tf_op jit(solution)/shard_map/reduce_scatter | solution.py:167
  1617.3 144.9 %copy-start.56 = (bf16[1,128,512]{1,2,0:T(8,128)(2,1)S(1)}, bf16[1,128,512]{1,2,0:T(8,128)(2,1)}, u32[]{:S(2)}) copy-start(bf16[1,128,512]{1,2,0:T(8,128)(2,1)} %copy-done.55) | copy-start | bytes 393220
  1825.8 298.3 %all-to-all-start.3 = ((bf16[6144,3,128]{2,1,0:T(4,128)(2,1)}), bf16[6144,3,128]{2,1,0:T(4,128)(2,1)}, u32[]{:S(2)}, u32[]{:S(2)}) async-start(bf16[6144,3,128]{2,1,0:T(4,128)(2,1)} %copy.417), calls=%async_computation.7 | async-start | bytes 12582912 | tf_op jit(solution)/shard_map/all_to_all | solution.py:340
  1831.8 228.6 %reduce-scatter.37.cloned.1.call-start = ((), (), s32[]{:S(2)}) async-start(), calls=%async_computation.34 | async-start | bytes 147456
  1836.4 254.9 %reduce-scatter.31.cloned.1.call-start = ((), (), s32[]{:S(2)}) async-start(), calls=%async_computation.27 | async-start | bytes 442368 | tf_op jit(solution)/shard_map/reduce_scatter | solution.py:161
  1844.4 278.1 %reduce-scatter.29.cloned.1.call-start = ((), (), s32[]{:S(2)}) async-start(), calls=%async_computation.25 | async-start | bytes 442368 | tf_op jit(solution)/shard_map/reduce_scatter | solution.py:161
  1897.0 134.5 %copy-start.115 = (f32[512]{0:T(512)S(1)}, f32[512]{0:T(512)}, u32[]{:S(2)}) copy-start(f32[512]{0:T(512)} %get-tuple-element.122) | copy-start | bytes 6148
  1897.0 134.5 %copy-start.116 = (f32[512]{0:T(512)S(1)}, f32[512]{0:T(512)}, u32[]{:S(2)}) copy-start(f32[512]{0:T(512)} %get-tuple-element.96) | copy-start | bytes 6148
  (119 other events, 1200.4 us)
Sparse Core Ops, SparseCore 0:
  403.3 70.1 reduce-scatter.20
  740.2 113.4 all-gather.14
  919.8 69.9 reduce-scatter.24
  992.6 70.2 reduce-scatter.22
  1071.2 70.2 all-gather.16
  1221.0 66.7 all-gather.30
  1317.1 72.8 all-gather.18
  1411.8 70.0 reduce-scatter.26
  1483.7 30.9 all-gather.32
  1516.4 70.1 all-gather.28
  1588.9 27.3 reduce-scatter.42
  1618.1 71.8 all-gather.26
  1692.0 70.1 all-gather.20
  1764.1 70.3 all-gather.24
  1837.2 26.5 reduce-scatter.38
  1865.9 28.9 reduce-scatter.40
  1896.8 71.9 all-gather.22
  1971.0 27.3 reduce-scatter.34
  2000.6 29.2 reduce-scatter.32
  2032.1 28.2 reduce-scatter.36
  2062.6 28.7 reduce-scatter.30
  2093.7 28.7 reduce-scatter.28
